TPU v7x, 256 devices: a whole 4x4x8 slice. The times are simulated.
256 devices in a mesh: tm: 32 (over x, y, core), space: 8 (over z).
Axes of the slice: x: 4, y: 4, z: 8, core: 2. Of those that a mesh axis runs over, the one named last changes fastest.
Arguments:
- snapshots: bfloat16 [512, 524288], P('tm', 'space'), may hold values from -6 to 6
- block_lists: int32 [8192, 2], P(('tm', 'space')), may hold values from 0 to 8191
- tile_counts: int32 [8192], P(('tm', 'space')), may hold values from 1 to 2
- remap_weights: bfloat16 [8192, 64, 128], P(('tm', 'space')), may hold values from -0.5 to 0.5
- basis: bfloat16 [524288, 1024], P(('tm', 'space')), may hold values from -6 to 6
- variances: float32 [1024], replicated, may hold values from 0.3 to 3
Outputs:
- coeffs: float32 [1024, 512], P('space')
- rotated: bfloat16 [524288, 1024], P(('tm', 'space'))
Inputs may be any that keep to these rules, and one draw needn't show every extreme that they name: `block_lists`: slots at or beyond a tile's count carry no weight.
All inputs are finite; a program needn't handle non-finite values.
Results may differ from a plain program's by a relative error of at most 0.0043.
Values may be sent and summed in bfloat16 or wider, within the bound.
No kernel may reach another device: no remote copies, remote signals or barrier semaphores. Data moves between devices by JAX's collectives and lax.ppermute only.
A program may use at most 192 MiB of HBM per device.

v0:
```python
import math
import jax
import jax.numpy as jnp
from jax import lax
from jax.sharding import PartitionSpec as P

TILE = 64
MAXB = 2


def per_device(snapshots, block_lists, tile_counts, remap_weights, basis, variances):
    local_tiles = block_lists.shape[0]
    time_rows = snapshots.shape[0]
    tm_size = lax.axis_size("tm")
    list_column, count_column = (
        lax.all_gather(block_lists, "tm", axis=0, tiled=True),
        lax.all_gather(tile_counts, "tm", axis=0, tiled=True),
    )
    gathered = lax.all_gather(snapshots, "space", axis=1, tiled=True)
    cell_total = gathered.shape[1]
    blocks = gathered.reshape(time_rows, cell_total // TILE, TILE)
    picked = blocks[:, list_column.reshape(-1), :].reshape(
        time_rows, tm_size * local_tiles, MAXB * TILE
    )
    slot_index = jnp.arange(MAXB * TILE, dtype=jnp.int32) // TILE
    weight_column = lax.all_gather(remap_weights, "tm", axis=0, tiled=True)
    keep = slot_index[None, :] < count_column[:, None]
    masked = jnp.where(keep[:, None, :], weight_column, jnp.zeros_like(weight_column))
    remap_part = jnp.einsum("kip,tkp->kit", masked, picked, preferred_element_type=jnp.float32)
    remap_part = remap_part.astype(jnp.bfloat16).reshape(tm_size, local_tiles * TILE, time_rows)
    arrived = lax.all_to_all(remap_part, "tm", split_axis=0, concat_axis=2, tiled=True)
    remapped = arrived.reshape(local_tiles * TILE, tm_size * time_rows)
    snap_total = remapped.shape[1]
    partial_coeffs = lax.dot_general(
        basis, remapped, (((0,), (0,)), ((), ())), preferred_element_type=jnp.float32
    )
    coeffs = lax.psum(partial_coeffs, ("tm", "space")) / math.sqrt(cell_total)
    coeff_half = coeffs.astype(jnp.bfloat16)
    coeff_rows = coeffs.shape[0] // lax.axis_size("space")
    own_coeffs = lax.dynamic_slice_in_dim(
        coeffs, lax.axis_index("space") * coeff_rows, coeff_rows, 0
    )
    update = lax.dot_general(
        remapped, coeff_half, (((1,), (1,)), ((), ())), preferred_element_type=jnp.float32
    ) / math.sqrt(snap_total)
    rotated = (basis.astype(jnp.float32) * variances[None, :] + update).astype(jnp.bfloat16)
    return (own_coeffs, rotated)


def solution(mesh):
    return jax.shard_map(
        per_device,
        mesh=mesh,
        in_specs=(
            P("tm", "space"),
            P(("tm", "space"), None),
            P(("tm", "space")),
            P(("tm", "space"), None, None),
            P(("tm", "space"), None),
            P(),
        ),
        out_specs=(P("space", None), P(("tm", "space"), None)),
        check_vma=False,
    )
```

profile of v0, /device:TPU:2, one launch (start us, length us, event | category | flops | bytes accessed | tf_op | source)
XLA Modules:
  0.0 671.5 jit_solution(16009837492111305055)
XLA Ops:
  7.2 0.7 all-gather.6.cloned.1.call-update
  7.9 0.7 all-gather.4.cloned.1.call-update
  8.7 24.3 %all-gather = s32[32,32,2]{1,2,0:T(2,128)S(1)} all-gather(s32[1,32,2]{1,2,0:T(2,128)} %bitcast.20), channel_id=1, replica_groups=mesh['tm'=32,'space'=8] {'tm'}, dimensions={0}, use_global_device_ids=true | all-gather | bytes 8448 | tf_op jit(solution)/shard_map/all_gather | solution.py:16
  33.0 0.3 copy.16
  33.2 0.3 reshape.86
  33.6 1.3 dynamic-slice
  35.5 0.9 dynamic-update-slice
  36.3 13.8 %all-reduce = s32[1024]{0:T(1024)S(1)} all-reduce(s32[1024]{0:T(1024)S(1)} %dynamic-update-slice), channel_id=1, replica_groups=mesh['tm'=32,'space'=8] {'tm'}, use_global_device_ids=true, to_apply=%add | all-reduce | flops 1024 | bytes 8192
  50.4 135.1 %all-gather.6.cloned.1.call-done = bf16[16,524288]{1,0:T(8,128)(2,1)} async-done(((bf16[16,65536]{1,0:T(8,128)(2,1)}), bf16[16,524288]{1,0:T(8,128)(2,1)}) %all-gather.6.cloned.1.call-update) | async-done | bytes 16777232 | tf_op jit(solution)/shard_map/all_gather | solution.py:19
  185.5 60.5 %reshape.85 = bf16[16,8192,64]{2,1,0:T(8,128)(2,1)} reshape(bf16[16,524288]{1,0:T(8,128)(2,1)} %all-gather.6.cloned.1.call-done) | data formatting | bytes 33554432 | tf_op jit(solution)/shard_map/reshape | solution.py:21
  246.0 29.6 %copy.17 = bf16[16,8192,64]{2,0,1:T(8,128)(2,1)} copy(bf16[16,8192,64]{2,1,0:T(8,128)(2,1)} %reshape.85) | data formatting | bytes 33554432 | tf_op jit(solution)/shard_map/reshape | solution.py:21
  275.6 33.4 %gather_fusion = bf16[2048,16,64]{2,1,0:T(8,128)(2,1)} fusion(bf16[16,8192,64]{2,0,1:T(8,128)(2,1)} %copy.17, s32[2048]{0:T(1024)S(1)} %broadcast_clamp_fusion), kind=kCustom, calls=%fused_computation | custom fusion | bytes 8396800 | tf_op jit(solution)/shard_map/gather | solution.py:22
  309.0 8.8 %copy.18 = bf16[16,2048,64]{2,1,0:T(8,128)(2,1)} copy(bf16[16,2048,64]{2,0,1:T(8,128)(2,1)} %bitcast.16) | data formatting | bytes 8388608 | tf_op jit(solution)/shard_map/gather | solution.py:22
  317.8 11.3 %reshape.87 = bf16[16,1024,128]{2,1,0:T(8,128)(2,1)} reshape(bf16[16,2048,64]{2,1,0:T(8,128)(2,1)} %copy.18) | data formatting | bytes 8388608 | tf_op jit(solution)/shard_map/reshape | solution.py:22
  329.1 14.3 %fusion.5 = bf16[1024,64,16]{1,2,0:T(8,128)(2,1)} fusion(bf16[16,1024,128]{2,1,0:T(8,128)(2,1)} %reshape.87, bf16[1024,64,128]{2,1,0:T(8,128)(2,1)} %all-gather.4.cloned.1.call-done, pred[1024,128]{1,0:T(8,128)(4,1)S(1)} %broadcast_compare_fusion), kind=kOutput, calls=%fused_computation.7 | convolution fusion | flops 277872640 | bytes 23199744 | tf_op jit(solution)/shard_map/kip,tkp->kit/dot_general | solution.py:29
  343.3 5.3 copy.20
  348.6 5.8 reshape.88
  354.4 1.2 copy.21
  355.5 32.6 %all_to_all.15 = bf16[32,2048,16]{1,2,0:T(8,128)(2,1)S(1)} all-to-all(bf16[32,2048,16]{1,2,0:T(8,128)(2,1)S(1)} %copy.21), channel_id=1, replica_groups=mesh['tm'=32,'space'=8] {'tm'}, dimensions={0} | all-to-all | bytes 4194304 | tf_op jit(solution)/shard_map/all_to_all | solution.py:31
  388.2 3.7 convolution_bitcast_fusion
  391.9 262.6 %all-reduce.3.cloned.1.call-done = f32[1024,512]{0,1:T(8,128)} async-done(((f32[1024,512]{0,1:T(8,128)}), f32[1024,512]{0,1:T(8,128)}) %all-reduce.3.cloned.1.call-update) | async-done | bytes 2097168 | tf_op jit(solution)/shard_map/psum | solution.py:37
  654.6 1.8 broadcast_multiply_fusion
  656.4 0.8 copy.22
  657.3 7.7 %add_convert_fusion = bf16[2048,1024]{1,0:T(8,128)(2,1)} fusion(bf16[2048,1024]{1,0:T(8,128)(2,1)} %param.10, bf16[2048,512]{0,1:T(8,128)(2,1)S(1)} %bitcast.18, f32[1024]{0:T(1024)S(1)} %copy-done.1, f32[1024,512]{0,1:T(8,128)} %all-reduce.3.cloned.1.call-done), kind=kOutput, calls=%fused_computation.4 | convolution fusion | flops 2159017984 | bytes 12587008 | tf_op jit(solution)/shard_map/dot_general | solution.py:43
  (15 shorter events, 0.4 us)
Async XLA Ops:
  7.2 178.3 %all-gather.6.cloned.1.call-start = ((), (), s32[]{:S(2)}) async-start(), calls=%async_computation.2 | async-start | bytes 18874368 | tf_op jit(solution)/shard_map/all_gather | solution.py:19
  7.9 321.2 %all-gather.4.cloned.1.call-start = ((), (), s32[]{:S(2)}) async-start(), calls=%async_computation.1 | async-start | bytes 17301504 | tf_op jit(solution)/shard_map/all_gather | solution.py:26
  8.6 645.9 %all-reduce.3.cloned.1.call-start = ((), (), s32[]{:S(2)}) async-start(), calls=%async_computation.3 | async-start | bytes 4194304 | tf_op jit(solution)/shard_map/psum | solution.py:37
  354.4 33.8 %copy-start = (bf16[2048,1024]{1,0:T(8,128)(2,1)S(1)}, bf16[2048,1024]{1,0:T(8,128)(2,1)}, u32[]{:S(2)}) copy-start(bf16[2048,1024]{1,0:T(8,128)(2,1)} %param.10) | copy-start | bytes 12582916
  391.9 265.4 %copy-start.1 = (f32[1024]{0:T(1024)S(1)}, f32[1024]{0:T(1024)}, u32[]{:S(2)}) copy-start(f32[1024]{0:T(1024)} %param.11) | copy-start | bytes 12292
Sparse Core Ops, SparseCore 0:
  9.8 175.6 all-gather.5
  188.0 76.1 all-gather.3
  392.0 262.4 all-reduce.2
where the time goes:
time: 673 us; the launch traced here: 671 us
  waiting for transfers between devices  399 us (59%)
  local copies, waits for them, and re-layouts  159 us (24%)
  blocking collectives  70.7 us (11%)
  matrix products  25.6 us (4%)
  between operations  14.5 us (2%)
    psum x1, waiting for transfers between devices, per_device(): coeffs = lax.psum(partial_coeffs, ('tm', 'space')) / math.sqrt(cell_total)  263 us
    all_gather x1, waiting for transfers between devices, per_device(): gathered = lax.all_gather(snapshots, 'space', axis=1, tiled=True)  135 us
    reshape x2, local copies, waits for them, and re-layouts, per_device(): blocks = gathered.reshape(time_rows, cell_total // TILE, TILE)  90.1 us
    gather x2, local copies, waits for them, and re-layouts, per_device(): blocks[:, list_column.reshape(-1), :]  42.2 us
    all_to_all x1, blocking collectives, per_device(): lax.all_to_all(remap_part, 'tm', split_axis=0, concat_axis=2, tiled=True)  32.6 us
    all_gather x1, blocking collectives, per_device(): lax.all_gather(block_lists, 'tm', axis=0, tiled=True)  24.3 us
    dot_general x1, matrix products, per_device(): jnp.einsum('kip,tkp->kit', masked, picked, preferred_element_type=jnp.flo...  14.3 us
    unnamed x1, blocking collectives  13.8 us
  transfers between devices with their start and end apart: 3, of which 2 were waited for; matrix products, arithmetic and copies ran while one was open for 22% of the time, Pallas kernels for 0%

commit v1 on v0

--- a/solution.py
+++ b/solution.py
@@ -34,7 +34,7 @@
     partial_coeffs = lax.dot_general(
         basis, remapped, (((0,), (0,)), ((), ())), preferred_element_type=jnp.float32
     )
-    coeffs = lax.psum(partial_coeffs, ("tm", "space")) / math.sqrt(cell_total)
+    coeffs = lax.psum(lax.psum(partial_coeffs, "tm"), "space") / math.sqrt(cell_total)
     coeff_half = coeffs.astype(jnp.bfloat16)
     coeff_rows = coeffs.shape[0] // lax.axis_size("space")
     own_coeffs = lax.dynamic_slice_in_dim(

time: 673 us -> 611 us (0.908)
  waiting for transfers between devices: 399 us -> 337 us
    psum x1 -> x2, waiting for transfers between devices: 263 us -> 200 us  [the longest x1 116 us: per_device(): lax.psum(partial_coeffs, 'tm')]
  transfers between devices with their start and end apart: 3 -> 4, of which waited for: 2 -> 3; matrix products, arithmetic and copies ran while one was open for 22% -> 24% of each run, Pallas kernels for 0% -> 0%
where the time goes in v1:
time: 611 us; the launch traced here: 610 us
  waiting for transfers between devices  337 us (55%)
  local copies, waits for them, and re-layouts  159 us (26%)
  blocking collectives  70.7 us (12%)
  matrix products  25.6 us (4%)
  between operations  14.5 us (2%)
    all_gather x1, waiting for transfers between devices, per_device(): gathered = lax.all_gather(snapshots, 'space', axis=1, tiled=True)  135 us
    psum x1, waiting for transfers between devices, per_device(): lax.psum(partial_coeffs, 'tm')  116 us
    reshape x2, local copies, waits for them, and re-layouts, per_device(): blocks = gathered.reshape(time_rows, cell_total // TILE, TILE)  90.1 us
    psum x1, waiting for transfers between devices, per_device(): lax.psum(lax.psum(partial_coeffs, 'tm'), 'space') / math.sqrt(cell_total)  84.8 us
    gather x2, local copies, waits for them, and re-layouts, per_device(): blocks[:, list_column.reshape(-1), :]  42.2 us
    all_to_all x1, blocking collectives, per_device(): lax.all_to_all(remap_part, 'tm', split_axis=0, concat_axis=2, tiled=True)  32.6 us
    all_gather x1, blocking collectives, per_device(): lax.all_gather(block_lists, 'tm', axis=0, tiled=True)  24.3 us
    dot_general x1, matrix products, per_device(): jnp.einsum('kip,tkp->kit', masked, picked, preferred_element_type=jnp.flo...  14.3 us
  transfers between devices with their start and end apart: 4, of which 3 were waited for; matrix products, arithmetic and copies ran while one was open for 24% of the time, Pallas kernels for 0%

profile of v1, /device:TPU:2, one launch (start us, length us, event | category | flops | bytes accessed | tf_op | source)
XLA Modules:
  0.0 609.5 jit_solution(7110356160714147768)
XLA Ops:
  7.2 0.7 all-gather.6.cloned.1.call-update
  7.9 0.7 all-gather.4.cloned.1.call-update
  8.7 24.3 %all-gather = s32[32,32,2]{1,2,0:T(2,128)S(1)} all-gather(s32[1,32,2]{1,2,0:T(2,128)} %bitcast.20), channel_id=1, replica_groups=mesh['tm'=32,'space'=8] {'tm'}, dimensions={0}, use_global_device_ids=true | all-gather | bytes 8448 | tf_op jit(solution)/shard_map/all_gather | solution.py:16
  33.2 0.3 reshape.86
  33.6 1.3 dynamic-slice
  35.5 0.9 dynamic-update-slice
  36.3 13.8 %all-reduce = s32[1024]{0:T(1024)S(1)} all-reduce(s32[1024]{0:T(1024)S(1)} %dynamic-update-slice), channel_id=1, replica_groups=mesh['tm'=32,'space'=8] {'tm'}, use_global_device_ids=true, to_apply=%add | all-reduce | flops 1024 | bytes 8192
  50.4 135.1 %all-gather.6.cloned.1.call-done = bf16[16,524288]{1,0:T(8,128)(2,1)} async-done(((bf16[16,65536]{1,0:T(8,128)(2,1)}), bf16[16,524288]{1,0:T(8,128)(2,1)}) %all-gather.6.cloned.1.call-update) | async-done | bytes 16777232 | tf_op jit(solution)/shard_map/all_gather | solution.py:19
  185.5 60.5 %reshape.85 = bf16[16,8192,64]{2,1,0:T(8,128)(2,1)} reshape(bf16[16,524288]{1,0:T(8,128)(2,1)} %all-gather.6.cloned.1.call-done) | data formatting | bytes 33554432 | tf_op jit(solution)/shard_map/reshape | solution.py:21
  246.0 29.6 %copy.17 = bf16[16,8192,64]{2,0,1:T(8,128)(2,1)} copy(bf16[16,8192,64]{2,1,0:T(8,128)(2,1)} %reshape.85) | data formatting | bytes 33554432 | tf_op jit(solution)/shard_map/reshape | solution.py:21
  275.6 33.4 %gather_fusion = bf16[2048,16,64]{2,1,0:T(8,128)(2,1)} fusion(bf16[16,8192,64]{2,0,1:T(8,128)(2,1)} %copy.17, s32[2048]{0:T(1024)S(1)} %broadcast_clamp_fusion), kind=kCustom, calls=%fused_computation | custom fusion | bytes 8396800 | tf_op jit(solution)/shard_map/gather | solution.py:22
  309.0 8.8 %copy.18 = bf16[16,2048,64]{2,1,0:T(8,128)(2,1)} copy(bf16[16,2048,64]{2,0,1:T(8,128)(2,1)} %bitcast.16) | data formatting | bytes 8388608 | tf_op jit(solution)/shard_map/gather | solution.py:22
  317.8 11.3 %reshape.87 = bf16[16,1024,128]{2,1,0:T(8,128)(2,1)} reshape(bf16[16,2048,64]{2,1,0:T(8,128)(2,1)} %copy.18) | data formatting | bytes 8388608 | tf_op jit(solution)/shard_map/reshape | solution.py:22
  329.1 14.3 %fusion.5 = bf16[1024,64,16]{1,2,0:T(8,128)(2,1)} fusion(bf16[16,1024,128]{2,1,0:T(8,128)(2,1)} %reshape.87, bf16[1024,64,128]{2,1,0:T(8,128)(2,1)} %all-gather.4.cloned.1.call-done, pred[1024,128]{1,0:T(8,128)(4,1)S(1)} %broadcast_compare_fusion), kind=kOutput, calls=%fused_computation.7 | convolution fusion | flops 277872640 | bytes 23199744 | tf_op jit(solution)/shard_map/kip,tkp->kit/dot_general | solution.py:29
  343.3 5.3 copy.20
  348.6 5.8 reshape.88
  354.4 1.2 copy.21
  355.5 32.6 %all_to_all.15 = bf16[32,2048,16]{1,2,0:T(8,128)(2,1)S(1)} all-to-all(bf16[32,2048,16]{1,2,0:T(8,128)(2,1)S(1)} %copy.21), channel_id=1, replica_groups=mesh['tm'=32,'space'=8] {'tm'}, dimensions={0} | all-to-all | bytes 4194304 | tf_op jit(solution)/shard_map/all_to_all | solution.py:31
  388.2 3.7 convolution_bitcast_fusion
  392.2 115.5 %all-reduce.4.cloned.1.call-done = f32[1024,512]{0,1:T(8,128)} async-done(((f32[1024,512]{0,1:T(8,128)}), f32[1024,512]{0,1:T(8,128)}) %all-reduce.4.cloned.1.call-update) | async-done | bytes 2097168 | tf_op jit(solution)/shard_map/psum | solution.py:37
  507.8 84.8 %all-reduce.6.cloned.1.call-done = f32[1024,512]{0,1:T(8,128)} async-done(((f32[1024,512]{0,1:T(8,128)}), f32[1024,512]{0,1:T(8,128)}) %all-reduce.6.cloned.1.call-update) | async-done | bytes 2097168 | tf_op jit(solution)/shard_map/psum | solution.py:37
  592.6 1.8 broadcast_multiply_fusion
  594.5 0.8 copy.22
  595.3 7.7 %add_convert_fusion = bf16[2048,1024]{1,0:T(8,128)(2,1)} fusion(bf16[2048,1024]{1,0:T(8,128)(2,1)} %param.10, bf16[2048,512]{0,1:T(8,128)(2,1)S(1)} %bitcast.18, f32[1024]{0:T(1024)S(1)} %copy-done.1, f32[1024,512]{0,1:T(8,128)} %all-reduce.6.cloned.1.call-done), kind=kOutput, calls=%fused_computation.4 | convolution fusion | flops 2159017984 | bytes 12587008 | tf_op jit(solution)/shard_map/dot_general | solution.py:43
  (18 shorter events, 1.0 us)
Async XLA Ops:
  7.2 178.3 %all-gather.6.cloned.1.call-start = ((), (), s32[]{:S(2)}) async-start(), calls=%async_computation.2 | async-start | bytes 18874368 | tf_op jit(solution)/shard_map/all_gather | solution.py:19
  7.9 321.2 %all-gather.4.cloned.1.call-start = ((), (), s32[]{:S(2)}) async-start(), calls=%async_computation.1 | async-start | bytes 17301504 | tf_op jit(solution)/shard_map/all_gather | solution.py:26
  8.6 499.1 %all-reduce.4.cloned.1.call-start = ((), (), s32[]{:S(2)}) async-start(), calls=%async_computation.3 | async-start | bytes 4194304 | tf_op jit(solution)/shard_map/psum | solution.py:37
  354.4 33.8 %copy-start = (bf16[2048,1024]{1,0:T(8,128)(2,1)S(1)}, bf16[2048,1024]{1,0:T(8,128)(2,1)}, u32[]{:S(2)}) copy-start(bf16[2048,1024]{1,0:T(8,128)(2,1)} %param.10) | copy-start | bytes 12582916
  391.9 203.4 %copy-start.1 = (f32[1024]{0:T(1024)S(1)}, f32[1024]{0:T(1024)}, u32[]{:S(2)}) copy-start(f32[1024]{0:T(1024)} %param.11) | copy-start | bytes 12292
  391.9 200.7 %all-reduce.6.cloned.1.call-start = ((), (), s32[]{:S(2)}) async-start(), calls=%async_computation.4 | async-start | bytes 4194304 | tf_op jit(solution)/shard_map/psum | solution.py:37
Sparse Core Ops, SparseCore 0:
  9.8 175.6 all-gather.5
  188.0 76.1 all-gather.3
  392.0 115.6 all-reduce.3
  510.0 82.5 all-reduce.5
